TPU v7x, 32 devices: a whole 2x2x4 slice. The times are simulated.
32 devices in a mesh: batch: 4 (over z), seq: 8 (over y, x, core).
Axes of the slice: x: 2, y: 2, z: 4, core: 2. Of those that a mesh axis runs over, the one named last changes fastest.
Arguments:
- inputs: float32 [8, 1024, 768], P('batch', 'seq'), may hold values from -6 to 6
- cotangent: float32 [8, 1024, 768], P('batch', 'seq'), may hold values from -6 to 6
- lengths: int32 [8], P('batch'), may hold values from 256 to 1024, as said below
- joint_weight: bfloat16 [768, 2304], P(('batch', 'seq')), may hold values from -0.3125 to 0.3125
- output_weight: bfloat16 [768, 768], P(('batch', 'seq')), may hold values from -1.25 to 1.25
- vectors: bfloat16 [8, 768], P(None, ('batch', 'seq')), may hold values from -2 to 2
- expand_weight: bfloat16 [768, 3072], P(('batch', 'seq')), may hold values from -0.21875 to 0.21875
- expand_bias: bfloat16 [3072], P(('batch', 'seq')), may hold values from -1.1953125 to 1.1953125
- reduce_weight: bfloat16 [3072, 768], P(('batch', 'seq')), may hold values from -0.15625 to 0.15625
Outputs:
- result: float32 [8, 1024, 768], P('batch', 'seq')
- grad_inputs: float32 [8, 1024, 768], P('batch', 'seq')
- grad_joint: float32 [768, 2304], P(('batch', 'seq'))
- grad_output: float32 [768, 768], P(('batch', 'seq'))
- grad_vectors: float32 [8, 768], P(None, ('batch', 'seq'))
- grad_expand: float32 [768, 3072], P(('batch', 'seq'))
- grad_expand_bias: float32 [3072], P(('batch', 'seq'))
- grad_reduce: float32 [3072, 768], P(('batch', 'seq'))
Inputs may be any that keep to these rules, and one draw needn't show every extreme that they name: `lengths`: some sequence is full (1024 valid tokens) in every draw.
All inputs are finite; a program needn't handle non-finite values.
Results may differ from a plain program's by a relative error of at most 0.018.
The roundings to bfloat16 on the way count: a program that leaves them out, or rounds other values in their place, can miss the bound.
Values may be sent and summed in bfloat16 or wider, within the bound.
A program may use at most 192 MiB of HBM per device.

v0:
```python
import math

import jax
import jax.numpy as jnp
from jax import lax
from jax.sharding import PartitionSpec as P

HEADS = 12
HEAD_DIM = 64


EPSILON = 1e-12
SCORE_SCALE = 0.125
NEG_FILL = -1e30
HALF_ROOT = 0.7071067811865476
INV_ROOT_TAU = 0.3989422804014327
block_limit = 256


def layer_norm(residual, norm_gain, norm_shift):
    centered = residual - jnp.mean(residual, axis=-1, keepdims=True)
    inverse = lax.rsqrt(jnp.mean(centered * centered, axis=-1, keepdims=True) + EPSILON)
    normed = centered * inverse
    return (normed * norm_gain + norm_shift, normed, inverse)


def norm_back(grad_out, normed, inverse, norm_gain):
    grad_normed = grad_out * norm_gain
    mean_grad = jnp.mean(grad_normed, axis=-1, keepdims=True)
    mean_proj = jnp.mean(grad_normed * normed, axis=-1, keepdims=True)
    grad_in = inverse * (grad_normed - mean_grad - normed * mean_proj)
    return (grad_in, jnp.sum(grad_out * normed, axis=0), jnp.sum(grad_out, axis=0))


def gelu_value(before_gelu):
    return 0.5 * before_gelu * (1.0 + lax.erf(before_gelu * HALF_ROOT))


def gelu_slope(before_gelu):
    return (
        0.5 * (1.0 + lax.erf(before_gelu * HALF_ROOT))
        + before_gelu * jnp.exp(-0.5 * before_gelu * before_gelu) * INV_ROOT_TAU
    )


def over_blocks(piece_rows, block_fn, carried):
    block_size = math.gcd(piece_rows, block_limit)

    def run_block(block_index, current):
        return block_fn(current, block_index * block_size, block_size)

    return lax.fori_loop(0, piece_rows // block_size, run_block, carried)


def head_scores(left_heads, right_heads, right_places, lengths):
    scores = (
        jnp.einsum("sqhd,skhd->shqk", left_heads, right_heads, preferred_element_type=jnp.float32)
        * SCORE_SCALE
    )
    allowed = right_places[None, :] < lengths[:, None]
    return jnp.where(allowed[:, None, None, :], scores, NEG_FILL)


def cut_heads(gathered_piece, offset, block_size, head_count):
    sliced = lax.dynamic_slice_in_dim(gathered_piece, offset, block_size, 1)
    return sliced.reshape(sliced.shape[0], block_size, head_count, -1)


def gather_attention(joint_weight, output_weight, vectors):
    return (
        lax.all_gather(joint_weight, ("batch", "seq"), axis=0, tiled=True),
        lax.all_gather(output_weight, ("batch", "seq"), axis=0, tiled=True),
        lax.all_gather(vectors, ("batch", "seq"), axis=1, tiled=True),
    )


def gather_feed(expand_weight, reduce_weight, expand_bias):
    return (
        lax.all_gather(expand_weight, ("batch", "seq"), axis=0, tiled=True),
        lax.all_gather(reduce_weight, ("batch", "seq"), axis=0, tiled=True),
        lax.all_gather(expand_bias, ("batch", "seq"), axis=0, tiled=True),
    )


def on_device(
    inputs,
    cotangent,
    lengths,
    joint_weight,
    output_weight,
    vectors,
    expand_weight,
    expand_bias,
    reduce_weight,
):
    seq_count, row_count, model_width = inputs.shape
    head_count = HEADS
    head_size = HEAD_DIM
    tokens = seq_count * row_count
    head_shape = (seq_count, row_count, head_count, head_size)
    own_places = lax.axis_index("seq") * row_count + jnp.arange(row_count, dtype=jnp.int32)
    row_valid = own_places[None, :] < lengths[:, None]
    row_mask = row_valid.reshape(tokens, 1).astype(jnp.float32)
    full_joint, full_output, full_vectors = gather_attention(joint_weight, output_weight, vectors)
    vector_rows = full_vectors.astype(jnp.float32)
    flat_inputs = inputs.reshape(tokens, model_width)
    input_low = flat_inputs.astype(jnp.bfloat16)
    projected = jnp.dot(input_low, full_joint, preferred_element_type=jnp.float32)
    query_low = (projected[:, :model_width] + vector_rows[2]).astype(jnp.bfloat16)
    key_low = projected[:, model_width : 2 * model_width].astype(jnp.bfloat16)
    value_low = (projected[:, 2 * model_width :] + vector_rows[3]).astype(jnp.bfloat16)
    query_heads = query_low.reshape(head_shape)
    key_rows = key_low.reshape(seq_count, row_count, model_width)
    value_rows = value_low.reshape(seq_count, row_count, model_width)
    start_state = (
        jnp.full((seq_count, head_count, row_count), NEG_FILL, jnp.float32),
        jnp.zeros((seq_count, head_count, row_count), jnp.float32),
        jnp.zeros(head_shape, jnp.float32),
    )
    key_piece = lax.all_gather(key_rows, "seq", axis=1, tiled=True)
    value_piece = lax.all_gather(value_rows, "seq", axis=1, tiled=True)

    def forward_score_block(current, offset, block_size):
        running_max, running_sum, summed = current
        key_heads = cut_heads(key_piece, offset, block_size, head_count)
        value_heads = cut_heads(value_piece, offset, block_size, head_count)
        key_places = offset + jnp.arange(block_size, dtype=jnp.int32)
        scores = head_scores(query_heads, key_heads, key_places, lengths)
        new_max = jnp.maximum(running_max, jnp.max(scores, axis=-1))
        factor = jnp.exp(running_max - new_max)
        exp_scores = jnp.exp(scores - new_max[..., None])
        running_sum = running_sum * factor + jnp.sum(exp_scores, axis=-1)
        update = jnp.einsum(
            "shqk,skhd->sqhd",
            exp_scores.astype(jnp.bfloat16),
            value_heads,
            preferred_element_type=jnp.float32,
        )
        summed = summed * jnp.transpose(factor, (0, 2, 1))[..., None] + update
        return (new_max, running_sum, summed)

    running_max, running_sum, summed = over_blocks(
        key_piece.shape[1], forward_score_block, start_state
    )
    attended = summed / jnp.transpose(running_sum, (0, 2, 1))[..., None]
    log_total = jnp.transpose(running_max + jnp.log(running_sum), (0, 2, 1))
    context_low = attended.reshape(tokens, model_width).astype(jnp.bfloat16)
    branch = jnp.dot(context_low, full_output, preferred_element_type=jnp.float32) + vector_rows[4]
    first, first_normed, first_inverse = layer_norm(
        flat_inputs + branch, vector_rows[0], vector_rows[1]
    )
    first_low = first.astype(jnp.bfloat16)
    full_expand, full_reduce, full_bias = gather_feed(expand_weight, reduce_weight, expand_bias)
    before_gelu = jnp.dot(
        first_low, full_expand, preferred_element_type=jnp.float32
    ) + full_bias.astype(jnp.float32)
    hidden_low = gelu_value(before_gelu).astype(jnp.bfloat16)
    feed = jnp.dot(hidden_low, full_reduce, preferred_element_type=jnp.float32) + vector_rows[7]
    result, second_normed, second_inverse = layer_norm(first + feed, vector_rows[5], vector_rows[6])
    full_expand, full_reduce, full_bias = gather_feed(expand_weight, reduce_weight, expand_bias)
    full_joint, full_output, full_vectors = gather_attention(joint_weight, output_weight, vectors)
    grad_res = cotangent.reshape(tokens, model_width) * row_mask
    grad_second, grad_gain_two, grad_shift_two = norm_back(
        grad_res, second_normed, second_inverse, vector_rows[5]
    )
    grad_feed_low = grad_second.astype(jnp.bfloat16)
    grad_reduce_local = jnp.dot(hidden_low.T, grad_feed_low, preferred_element_type=jnp.float32)
    grad_hidden = jnp.dot(
        grad_feed_low, full_reduce.T, preferred_element_type=jnp.float32
    ) * gelu_slope(before_gelu)
    grad_hidden_low = grad_hidden.astype(jnp.bfloat16)
    grad_expand_local = jnp.dot(first_low.T, grad_hidden_low, preferred_element_type=jnp.float32)
    grad_bias_local = jnp.sum(grad_hidden_low.astype(jnp.float32), axis=0)
    grad_first = grad_second + jnp.dot(
        grad_hidden_low, full_expand.T, preferred_element_type=jnp.float32
    )
    grad_resid, grad_gain_one, grad_shift_one = norm_back(
        grad_first, first_normed, first_inverse, vector_rows[0]
    )
    grad_branch_low = grad_resid.astype(jnp.bfloat16)
    grad_output_local = jnp.dot(context_low.T, grad_branch_low, preferred_element_type=jnp.float32)
    grad_context_low = jnp.dot(
        grad_branch_low, full_output.T, preferred_element_type=jnp.float32
    ).astype(jnp.bfloat16)
    grad_context_heads = grad_context_low.reshape(head_shape)
    row_delta = jnp.sum(grad_context_heads.astype(jnp.float32) * attended, axis=-1)
    log_heads = jnp.transpose(log_total, (0, 2, 1))
    delta_heads = jnp.transpose(row_delta, (0, 2, 1))
    query_key_piece = lax.all_gather(key_rows, "seq", axis=1, tiled=True)
    query_value_piece = lax.all_gather(value_rows, "seq", axis=1, tiled=True)

    def query_score_block(current, offset, block_size):
        key_heads = cut_heads(query_key_piece, offset, block_size, head_count)
        value_heads = cut_heads(query_value_piece, offset, block_size, head_count)
        key_places = offset + jnp.arange(block_size, dtype=jnp.int32)
        scores = head_scores(query_heads, key_heads, key_places, lengths)
        softmax_rows = jnp.exp(scores - log_heads[..., None])
        grad_probs = jnp.einsum(
            "sqhd,skhd->shqk", grad_context_heads, value_heads, preferred_element_type=jnp.float32
        )
        grad_scores = (softmax_rows * (grad_probs - delta_heads[..., None])).astype(jnp.bfloat16)
        return (
            current
            + jnp.einsum(
                "shqk,skhd->sqhd", grad_scores, key_heads, preferred_element_type=jnp.float32
            )
            * SCORE_SCALE
        )

    grad_query = over_blocks(
        query_key_piece.shape[1], query_score_block, jnp.zeros(head_shape, jnp.float32)
    )
    own_keys = key_low.reshape(head_shape)
    own_values = value_low.reshape(head_shape)
    query_rows = query_low.reshape(seq_count, row_count, model_width)
    grad_context_rows = grad_context_low.reshape(seq_count, row_count, model_width)
    zero_heads = jnp.zeros(head_shape, jnp.float32)
    query_piece = lax.all_gather(query_rows.astype(jnp.float32), "seq", axis=1, tiled=True).astype(
        jnp.bfloat16
    )
    grad_piece = lax.all_gather(
        grad_context_rows.astype(jnp.float32), "seq", axis=1, tiled=True
    ).astype(jnp.bfloat16)
    log_piece = lax.all_gather(log_total, "seq", axis=1, tiled=True)
    delta_piece = lax.all_gather(row_delta, "seq", axis=1, tiled=True)

    def key_score_block(current, offset, block_size):
        grad_key, grad_value = current
        query_block = cut_heads(query_piece, offset, block_size, head_count)
        grad_block = cut_heads(grad_piece, offset, block_size, head_count)
        log_block = jnp.transpose(
            lax.dynamic_slice_in_dim(log_piece, offset, block_size, 1), (0, 2, 1)
        )
        delta_block = jnp.transpose(
            lax.dynamic_slice_in_dim(delta_piece, offset, block_size, 1), (0, 2, 1)
        )
        scores = head_scores(query_block, own_keys, own_places, lengths)
        softmax_rows = jnp.exp(scores - log_block[..., None])
        grad_value = grad_value + jnp.einsum(
            "shqk,sqhd->skhd",
            softmax_rows.astype(jnp.bfloat16),
            grad_block,
            preferred_element_type=jnp.float32,
        )
        grad_probs = jnp.einsum(
            "sqhd,skhd->shqk", grad_block, own_values, preferred_element_type=jnp.float32
        )
        grad_scores = (softmax_rows * (grad_probs - delta_block[..., None])).astype(jnp.bfloat16)
        grad_key = (
            grad_key
            + jnp.einsum(
                "shqk,sqhd->skhd", grad_scores, query_block, preferred_element_type=jnp.float32
            )
            * SCORE_SCALE
        )
        return (grad_key, grad_value)

    grad_key, grad_value = over_blocks(
        query_piece.shape[1], key_score_block, (zero_heads, zero_heads)
    )
    grad_query_low = grad_query.reshape(tokens, model_width).astype(jnp.bfloat16)
    grad_key_low = grad_key.reshape(tokens, model_width).astype(jnp.bfloat16)
    grad_value_low = grad_value.reshape(tokens, model_width).astype(jnp.bfloat16)
    grad_projected = jnp.concatenate([grad_query_low, grad_key_low, grad_value_low], axis=1)
    grad_joint_local = jnp.dot(input_low.T, grad_projected, preferred_element_type=jnp.float32)
    grad_inputs = grad_resid + jnp.dot(
        grad_projected, full_joint.T, preferred_element_type=jnp.float32
    )
    grad_vector_local = jnp.stack(
        [
            grad_gain_one,
            grad_shift_one,
            jnp.sum(grad_query_low.astype(jnp.float32), axis=0),
            jnp.sum(grad_value_low.astype(jnp.float32), axis=0),
            jnp.sum(grad_branch_low.astype(jnp.float32), axis=0),
            grad_gain_two,
            grad_shift_two,
            jnp.sum(grad_feed_low.astype(jnp.float32), axis=0),
        ],
        axis=0,
    )
    every_grad = (
        lax.psum_scatter(grad_joint_local, ("batch", "seq"), scatter_dimension=0, tiled=True),
        lax.psum_scatter(grad_output_local, ("batch", "seq"), scatter_dimension=0, tiled=True),
        lax.psum_scatter(grad_vector_local, ("batch", "seq"), scatter_dimension=1, tiled=True),
        lax.psum_scatter(grad_expand_local, ("batch", "seq"), scatter_dimension=0, tiled=True),
        lax.psum_scatter(grad_reduce_local, ("batch", "seq"), scatter_dimension=0, tiled=True),
        lax.psum_scatter(grad_bias_local, ("batch", "seq"), scatter_dimension=0, tiled=True),
    )
    summed_grads = (
        every_grad[0],
        every_grad[1],
        every_grad[2],
        every_grad[3],
        every_grad[5],
        every_grad[4],
    )
    return (
        result.reshape(seq_count, row_count, model_width),
        grad_inputs.reshape(seq_count, row_count, model_width),
        summed_grads[0],
        summed_grads[1],
        summed_grads[2],
        summed_grads[3],
        summed_grads[4],
        summed_grads[5],
    )


def solution(mesh):
    return jax.shard_map(
        on_device,
        mesh=mesh,
        in_specs=(
            P("batch", "seq", None),
            P("batch", "seq", None),
            P("batch"),
            P(("batch", "seq"), None),
            P(("batch", "seq"), None),
            P(None, ("batch", "seq")),
            P(("batch", "seq"), None),
            P(("batch", "seq")),
            P(("batch", "seq"), None),
        ),
        out_specs=(
            P("batch", "seq", None),
            P("batch", "seq", None),
            P(("batch", "seq"), None),
            P(("batch", "seq"), None),
            P(None, ("batch", "seq")),
            P(("batch", "seq"), None),
            P(("batch", "seq")),
            P(("batch", "seq"), None),
        ),
        check_vma=False,
    )
```

profile of v0, /device:TPU:0, one launch (start us, length us, event | category | flops | bytes accessed | tf_op | source)
XLA Modules:
  0.0 933.9 jit_solution(14947603904513098469)
XLA Ops:
  9.1 64.5 %all-gather.10.cloned.1.call-done = bf16[768,2304]{1,0:T(8,128)(2,1)} async-done(((bf16[24,2304]{1,0:T(8,128)(2,1)}), bf16[768,2304]{1,0:T(8,128)(2,1)}) %all-gather.10.cloned.1.call-update) | async-done | bytes 3538960 | tf_op jit(solution)/shard_map/all_gather | solution.py:71
  77.9 42.5 %all-gather = bf16[32,24,8]{1,2,0:T(8,128)(2,1)} all-gather(bf16[1,24,8]{1,2,0:T(8,128)(2,1)S(1)} %bitcast.230), channel_id=1, replica_groups=mesh['batch'=4,'seq'=8] {'batch','seq'}, dimensions={0}, use_global_device_ids=true | all-gather | bytes 12672 | tf_op jit(solution)/shard_map/all_gather | solution.py:73
  131.3 37.1 %all-reduce = bf16[3072]{0:T(1024)(128)(2,1)S(1)} all-reduce(bf16[3072]{0:T(1024)(128)(2,1)S(1)} %dynamic-update-slice), channel_id=1, replica_groups=mesh['batch'=4,'seq'=8] {'batch','seq'}, use_global_device_ids=true, to_apply=%add | all-reduce | flops 3072 | bytes 12288
  175.0 38.4 %while.48 = (s32[]{:T(128)}, f32[2,12,128]{2,1,0:T(8,128)S(1)}, f32[2,12,128]{2,1,0:T(8,128)}, f32[2,128,12,64]{1,3,2,0:T(8,128)}, s32[2]{0:T(128)}, /*index=5*/...) while((s32[]{:T(128)}, f32[2,12,128]{2,1,0:T(8,128)S(1)}, ...), condition=%wide.region_3.4_spmd.clone, body=%wide.region_0.3_spmd.clone.sunk | while | flops 210586368 | bytes 25862536 | solution.py:52
  219.4 60.8 %all-gather.18.cloned.1.call-done = bf16[768,3072]{1,0:T(8,128)(2,1)} async-done(((bf16[24,3072]{1,0:T(8,128)(2,1)}), bf16[768,3072]{1,0:T(8,128)(2,1)}) %all-gather.18.cloned.1.call-update) | async-done | bytes 4718608 | tf_op jit(solution)/shard_map/all_gather | solution.py:79
  280.2 6.1 multiply_convert_fusion.2
  286.3 59.1 %all-gather.20.cloned.1.call-done = bf16[3072,768]{1,0:T(8,128)(2,1)} async-done(((bf16[96,768]{1,0:T(8,128)(2,1)}), bf16[3072,768]{1,0:T(8,128)(2,1)}) %all-gather.20.cloned.1.call-update) | async-done | bytes 4718608 | tf_op jit(solution)/shard_map/all_gather | solution.py:80
  345.5 4.4 fusion.75
  362.9 6.7 fusion.70
  375.6 5.1 fusion.66
  380.8 34.9 %while.49 = (s32[]{:T(128)}, f32[2,128,12,64]{1,3,2,0:T(8,128)}, bf16[2,1024,768]{1,2,0:T(8,128)(2,1)}, s32[2]{0:T(128)}, bf16[2,128,12,64]{1,3,2,0:T(8,128)(2,1...) while((s32[]{:T(128)}, f32[2,128,12,64]{1,3,2,0:T(8,128)}, ...), condition=%wide.region_14.15_spmd.clone, body=%wide.region_13.14_spmd.clone.sunk | while | flops 307299072 | bytes 17329384 | solution.py:52
  411.4 4.2 fusion.148
  418.0 10.1 %all_gather.53 = f32[2,1024,12]{1,0,2:T(2,128)} all-gather(f32[2,128,12]{1,0,2:T(2,128)S(1)} %copy-done.29), channel_id=1, replica_groups=mesh['batch'=4,'seq'=8] {'seq'}, dimensions={1}, use_global_device_ids=true | all-gather | bytes 110592 | tf_op jit(solution)/shard_map/all_gather | solution.py:225
  428.1 10.4 %all_gather.51 = f32[2,1024,12]{1,2,0:T(8,128)} all-gather(f32[2,128,12]{1,2,0:T(8,128)} %bitcast.229), channel_id=1, replica_groups=mesh['batch'=4,'seq'=8] {'seq'}, dimensions={1}, use_global_device_ids=true | all-gather | bytes 110592 | tf_op jit(solution)/shard_map/all_gather | solution.py:224
  439.3 57.5 %while.50 = (s32[]{:T(128)}, f32[2,128,12,64]{1,3,2,0:T(8,128)}, f32[2,128,12,64]{1,3,2,0:T(8,128)}, bf16[2,1024,768]{1,2,0:T(8,128)(2,1)}, s32[2]{0:T(128)}, /*...) while((s32[]{:T(128)}, f32[2,128,12,64]{1,3,2,0:T(8,128)}, ...), condition=%wide.region_16.17_spmd.clone, body=%wide.region_15.16_spmd.clone.sunk | while | flops 411500928 | bytes 24602652 | solution.py:52
  445.5 4.7 fusion.157
  459.5 4.9 fusion.157
  474.0 4.9 fusion.157
  488.5 4.9 fusion.157
  504.4 8.1 copy.96
  513.4 40.3 %all-reduce.3 = (f32[8,768]{1,0:T(8,128)S(1)}, f32[3072]{0:T(1024)S(1)}) all-reduce(f32[8,768]{1,0:T(8,128)S(1)} %stack.35, f32[3072]{0:T(1024)S(1)} %copy-done.41), channel_id=4, replica_groups=mesh['batch'=4,'seq'=8] {'batch','seq'}, use_global_device_ids=true, to_apply=%region_27.28.clone | all-reduce | flops 9216 | bytes 73728
  559.2 101.4 %reduce-scatter.10.cloned.1.call-done = f32[24,3072]{1,0:T(8,128)} async-done(((f32[768,3072]{1,0:T(8,128)}), f32[24,3072]{1,0:T(8,128)}) %reduce-scatter.10.cloned.1.call-update) | async-done | bytes 294928 | tf_op jit(solution)/shard_map/reduce_scatter | solution.py:286
  660.6 140.9 %reduce-scatter.12.cloned.1.call-done = f32[96,768]{1,0:T(8,128)} async-done(((f32[3072,768]{1,0:T(8,128)}), f32[96,768]{1,0:T(8,128)}) %reduce-scatter.12.cloned.1.call-update) | async-done | bytes 294928 | tf_op jit(solution)/shard_map/reduce_scatter | solution.py:287
  801.5 125.5 %reduce-scatter.14.cloned.1.call-done = f32[24,2304]{1,0:T(8,128)} async-done(((f32[768,2304]{1,0:T(8,128)}), f32[24,2304]{1,0:T(8,128)}) %reduce-scatter.14.cloned.1.call-update) | async-done | bytes 221200
  (361 shorter events, 171.9 us)
Async XLA Ops:
  7.2 66.5 %all-gather.10.cloned.1.call-start = ((), (), s32[]{:S(2)}) async-start(), calls=%async_computation.4 | async-start | bytes 3649536 | tf_op jit(solution)/shard_map/all_gather | solution.py:71
  7.9 167.1 %all-gather.12.cloned.1.call-start = ((), (), s32[]{:S(2)}) async-start(), calls=%async_computation.5 | async-start | bytes 3538944 | tf_op jit(solution)/shard_map/all_gather | solution.py:120
  9.1 64.6 %copy-start.9 = (bf16[256,768]{1,0:T(8,128)(2,1)}, bf16[256,768]{1,0:T(8,128)(2,1)S(1)}, u32[]{:S(2)}) copy-start(bf16[256,768]{1,0:T(8,128)(2,1)S(1)} %bitcast_convert_fusion) | copy-start | bytes 1179652
  9.1 68.7 %copy-start.47 = (bf16[8,24]{1,0:T(8,128)(2,1)S(1)}, bf16[8,24]{1,0:T(8,128)(2,1)}, u32[]{:S(2)}) copy-start(bf16[8,24]{1,0:T(8,128)(2,1)} %param.20) | copy-start | bytes 1156
  76.8 93.5 %copy-start.4 = (f32[2,128,768]{2,1,0:T(8,128)S(1)}, f32[2,128,768]{2,1,0:T(8,128)}, u32[]{:S(2)}) copy-start(f32[2,128,768]{2,1,0:T(8,128)} %param.16) | copy-start | bytes 2359300
  76.8 49.9 %copy-start.14 = (bf16[256,768]{1,0:T(8,128)(2,1)}, bf16[256,768]{1,0:T(8,128)(2,1)S(1)}, u32[]{:S(2)}) copy-start(bf16[256,768]{1,0:T(8,128)(2,1)S(1)} %slice.73) | copy-start | bytes 1179652
  77.8 97.2 %all-gather.14.cloned.1.call-start = ((), (), s32[]{:S(2)}) async-start(), calls=%async_computation.6 | async-start | bytes 3538944 | tf_op jit(solution)/shard_map/all_gather | solution.py:121
  127.7 47.3 %copy-start.11 = (bf16[256,768]{1,0:T(8,128)(2,1)}, bf16[256,768]{1,0:T(8,128)(2,1)S(1)}, u32[]{:S(2)}) copy-start(bf16[256,768]{1,0:T(8,128)(2,1)S(1)} %get-tuple-element.821) | copy-start | bytes 1179652
  127.7 46.1 %copy-start.13 = (bf16[256,768]{1,0:T(8,128)(2,1)S(1)}, bf16[256,768]{1,0:T(8,128)(2,1)}, u32[]{:S(2)}) copy-start(bf16[256,768]{1,0:T(8,128)(2,1)} %get-tuple-element.822) | copy-start | bytes 1179652
  128.6 88.4 %all-gather.16.cloned.1.call-start = ((), (), s32[]{:S(2)}) async-start(), calls=%async_computation.7 | async-start | bytes 1216512 | tf_op jit(solution)/shard_map/all_gather | solution.py:72
  129.2 151.0 %all-gather.18.cloned.1.call-start = ((), (), s32[]{:S(2)}) async-start(), calls=%async_computation.8 | async-start | bytes 4866048 | tf_op jit(solution)/shard_map/all_gather | solution.py:79
  129.8 215.7 %all-gather.20.cloned.1.call-start = ((), (), s32[]{:S(2)}) async-start(), calls=%async_computation.9 | async-start | bytes 4866048 | tf_op jit(solution)/shard_map/all_gather | solution.py:80
  130.4 308.9 %all-gather.22.cloned.1.call-start = ((), (), s32[]{:S(2)}) async-start(), calls=%async_computation.10 | async-start | bytes 3538944 | tf_op jit(solution)/shard_map/all_gather | solution.py:218
  174.7 264.6 %all-gather.24.cloned.1.call-start = ((), (), s32[]{:S(2)}) async-start(), calls=%async_computation.11 | async-start | bytes 3538944 | tf_op jit(solution)/shard_map/all_gather | solution.py:221
  213.4 66.8 %copy-start.27 = (f32[768]{0:T(1024)S(1)}, f32[768]{0:T(1024)}, u32[]{:S(2)}) copy-start(f32[768]{0:T(1024)} %get-tuple-element.737) | copy-start | bytes 9220
  213.4 66.8 %copy-start.30 = (f32[768]{0:T(1024)S(1)}, f32[768]{0:T(1024)}, u32[]{:S(2)}) copy-start(f32[768]{0:T(1024)} %get-tuple-element.736) | copy-start | bytes 9220
  213.4 66.8 %copy-start.40 = (f32[3072]{0:T(1024)S(1)}, f32[3072]{0:T(1024)}, u32[]{:S(2)}) copy-start(f32[3072]{0:T(1024)} %convert_element_type.147) | copy-start | bytes 36868
  219.2 139.1 %copy-start.33 = (f32[256]{0:T(256)}, f32[256]{0:T(256)S(1)}, u32[]{:S(2)}) copy-start(f32[256]{0:T(256)S(1)} %broadcast_multiply_fusion.4) | copy-start | bytes 3076
  219.4 138.9 %copy-start.39 = (f32[256]{0:T(256)}, f32[256]{0:T(256)S(1)}, u32[]{:S(2)}) copy-start(f32[256]{0:T(256)S(1)} %add_rsqrt_fusion.1) | copy-start | bytes 3076
  280.2 65.2 %copy-start.44 = (f32[768]{0:T(1024)S(1)}, f32[768]{0:T(1024)}, u32[]{:S(2)}) copy-start(f32[768]{0:T(1024)} %get-tuple-element.735) | copy-start | bytes 9220
  360.6 198.6 %reduce-scatter.8.cloned.1.call-start = ((), (), s32[]{:S(2)}) async-start(), calls=%async_computation.12 | async-start | bytes 2433024 | tf_op jit(solution)/shard_map/reduce_scatter | solution.py:284
  362.6 298.0 %reduce-scatter.10.cloned.1.call-start = ((), (), s32[]{:S(2)}) async-start(), calls=%async_computation.13 | async-start | bytes 9732096 | tf_op jit(solution)/shard_map/reduce_scatter | solution.py:286
  369.6 432.0 %reduce-scatter.12.cloned.1.call-start = ((), (), s32[]{:S(2)}) async-start(), calls=%async_computation.14 | async-start | bytes 9732096 | tf_op jit(solution)/shard_map/reduce_scatter | solution.py:287
  380.7 546.3 %reduce-scatter.14.cloned.1.call-start = ((), (), s32[]{:S(2)}) async-start(), calls=%async_computation.15 | async-start | bytes 7299072
  (71 other events, 247.8 us)
Sparse Core Ops, SparseCore 0:
  10.9 62.7 all-gather.9
  77.9 31.7 all-gather.11
  128.7 29.0 all-gather.13
  160.6 54.1 all-gather.15
  217.6 62.5 all-gather.17
  283.0 62.4 all-gather.19
  347.3 31.6 all-gather.21
  380.9 32.8 all-gather.23
  419.6 99.0 reduce-scatter.7
  526.0 134.5 reduce-scatter.9
  667.1 134.4 reduce-scatter.11
  808.6 118.3 reduce-scatter.13
where the time goes:
time: 937 us; the launch traced here: 934 us
  waiting for transfers between devices  555 us (59%)
  blocking collectives  140 us (15%)
  matrix products  108 us (12%)
  local copies, waits for them, and re-layouts  76 us (8%)
  other arithmetic  39 us (4%)
  between operations  14.8 us (2%)
    reduce_scatter x1, waiting for transfers between devices, on_device(): lax.psum_scatter(grad_reduce_local, ('batch', 'seq'), scatter_dimension=0...  141 us
    unnamed x13, waiting for transfers between devices  128 us
    reduce_scatter x1, waiting for transfers between devices, on_device(): lax.psum_scatter(grad_expand_local, ('batch', 'seq'), scatter_dimension=0...  101 us
    unnamed x2, blocking collectives  77.4 us
    all_gather x1, waiting for transfers between devices, gather_attention(): lax.all_gather(joint_weight, ('batch', 'seq'), axis=0, tiled=True)  64.5 us
    all_gather x1, waiting for transfers between devices, gather_feed(): lax.all_gather(expand_weight, ('batch', 'seq'), axis=0, tiled=True)  60.8 us
    all_gather x1, waiting for transfers between devices, gather_feed(): lax.all_gather(reduce_weight, ('batch', 'seq'), axis=0, tiled=True)  59.1 us
    all_gather x1, blocking collectives, gather_attention(): lax.all_gather(vectors, ('batch', 'seq'), axis=1, tiled=True)  42.5 us
  transfers between devices with their start and end apart: 12, of which 6 were waited for; matrix products, arithmetic and copies ran while one was open for 22% of the time, Pallas kernels for 0%

commit v1 on v0

--- a/solution.py
+++ b/solution.py
@@ -3,6 +3,8 @@
 import jax
 import jax.numpy as jnp
 from jax import lax
+from jax.experimental import pallas as pl
+from jax.experimental.pallas import tpu as pltpu
 from jax.sharding import PartitionSpec as P
 
 HEADS = 12
@@ -82,7 +84,7 @@
     )
 
 
-def on_device(
+def general_on_device(
     inputs,
     cotangent,
     lengths,
@@ -307,30 +309,1151 @@
     )
 
 
+MESH = pl.DeviceIdType.MESH
+ANY = pl.BlockSpec(memory_space=pl.ANY)
+VM = pl.BlockSpec(memory_space=pltpu.VMEM)
+SM = pl.BlockSpec(memory_space=pltpu.SMEM)
+DMA = pltpu.SemaphoreType.DMA
+VMEM_LIMIT = 60 << 20
+F32 = jnp.float32
+BF16 = jnp.bfloat16
+
+
+def send(src, dst, send_sem, recv_sem, device):
+    return pltpu.make_async_remote_copy(
+        src_ref=src,
+        dst_ref=dst,
+        send_sem=send_sem,
+        recv_sem=recv_sem,
+        device_id=device,
+        device_id_type=MESH,
+    )
+
+
+class Place:
+    def __init__(self, nb):
+        self.nb = nb
+        self.b = lax.axis_index("batch")
+        self.s = lax.axis_index("seq")
+        self.c = self.s % 2
+        self.p = self.s // 2
+        x, y = self.p % 2, self.p // 2
+        self.px = 2 * y + (1 - x)
+        self.py = 2 * (1 - y) + x
+        self.pd = 2 * (1 - y) + (1 - x)
+        self.sib = (self.b, 2 * self.p + 1 - self.c)
+        self.xn = (self.b, 2 * self.px + self.c)
+        self.yn = (self.b, 2 * self.py + self.c)
+
+    def chip(self, step):
+        return (self.p, self.px, self.py, self.pd)[step]
+
+    def up(self, step):
+        return (self.b + step) % self.nb
+
+    def down(self, step):
+        return (self.b + self.nb - step) % self.nb
+
+
+def greet(devices):
+    barrier = pltpu.get_barrier_semaphore()
+    for device in devices:
+        pl.semaphore_signal(barrier, inc=1, device_id=device, device_id_type=MESH)
+    pl.semaphore_wait(barrier, len(devices))
+
+
+def same_core(pos):
+    return [
+        (pos.up(d), 2 * pos.chip(k) + pos.c)
+        for d in range(pos.nb)
+        for k in range(4)
+        if d or k
+    ]
+
+
+def plane_others(pos):
+    return [
+        (pos.b, 2 * pos.chip(k) + (pos.c if j == 0 else 1 - pos.c))
+        for k in range(4)
+        for j in range(2)
+        if k or j
+    ]
+
+
+class Gather:
+    SEMS = 6
+
+    def __init__(self, pos, shard, out, halves, sems):
+        self.pos, self.shard, self.out, self.halves = pos, shard, out, halves
+        self.zs, self.xs, self.ys, self.f0, self.f1, self.sb = sems[:6]
+        self.started = []
+
+    @staticmethod
+    def scratch(nb):
+        return [DMA((2, nb)) for _ in range(6)]
+
+    def src(self, k):
+        pos = self.pos
+        return self.shard if k == 0 else self.out.at[pos.down(k), pos.p, pos.c]
+
+    def z_copy(self, k):
+        pos = self.pos
+        return send(
+            self.shard,
+            self.out.at[pos.b, pos.p, pos.c],
+            self.zs.at[0, k],
+            self.zs.at[1, k],
+            (pos.up(k), pos.s),
+        )
+
+    def z_land(self, k):
+        pos = self.pos
+        land = self.out.at[pos.down(k), pos.p, pos.c]
+        return send(land, land, self.zs.at[0, k], self.zs.at[1, k], (pos.up(k), pos.s))
+
+    def go(self, copy):
+        copy.start()
+        self.started.append(copy)
+
+    def own(self, local_sem):
+        pos = self.pos
+        for k in range(1, pos.nb):
+            self.go(self.z_copy(k))
+        self.local = pltpu.make_async_copy(
+            self.shard, self.out.at[pos.b, pos.p, pos.c], local_sem
+        )
+        self.local.start()
+
+    def plane(self, k):
+        pos = self.pos
+        if k:
+            self.z_land(k).wait_recv()
+        src, there = self.src(k), self.out.at[pos.down(k), pos.p, pos.c]
+        self.go(send(src, there, self.xs.at[0, k], self.xs.at[1, k], pos.xn))
+        self.go(send(src, there, self.ys.at[0, k], self.ys.at[1, k], pos.yn))
+
+    def land(self, sems, k, chip, half=None):
+        pos = self.pos
+        ref = self.out.at[pos.down(k), chip, pos.c]
+        if half is not None:
+            ref = ref.at[half]
+        return send(ref, ref, sems.at[0, k], sems.at[1, k], pos.xn)
+
+    def forward(self, k):
+        pos = self.pos
+        h0, h1 = self.halves
+        self.land(self.xs, k, pos.px).wait_recv()
+        ref = self.out.at[pos.down(k), pos.px, pos.c].at[h0]
+        self.go(send(ref, ref, self.f0.at[0, k], self.f0.at[1, k], pos.yn))
+        self.land(self.ys, k, pos.py).wait_recv()
+        if h1 is not None:
+            ref = self.out.at[pos.down(k), pos.py, pos.c].at[h1]
+            self.go(send(ref, ref, self.f1.at[0, k], self.f1.at[1, k], pos.xn))
+
+    def sibling(self, k):
+        pos = self.pos
+        h0, h1 = self.halves
+        self.land(self.f0, k, pos.pd, h0).wait_recv()
+        if h1 is not None:
+            self.land(self.f1, k, pos.pd, h1).wait_recv()
+        if k == 0:
+            self.local.wait()
+        ref = self.out.at[pos.down(k), :, pos.c]
+        self.go(send(ref, ref, self.sb.at[0, k], self.sb.at[1, k], pos.sib))
+
+    def finish(self):
+        pos = self.pos
+        for k in range(pos.nb):
+            ref = self.out.at[pos.down(k), :, 1 - pos.c]
+            send(ref, ref, self.sb.at[0, k], self.sb.at[1, k], pos.sib).wait_recv()
+        for copy in self.started:
+            copy.wait_send()
+
+
+class InputExchange:
+    def __init__(self, pos, rows, out, sems):
+        self.pos, self.rows, self.out, self.sems = pos, rows, out, sems
+        self.started = []
+
+    @staticmethod
+    def scratch():
+        return [DMA((2, 2)), DMA((2, 2)), DMA((2, 2)), DMA((2,)), DMA]
+
+    def go(self, copy):
+        copy.start()
+        self.started.append(copy)
+
+    def start(self):
+        pos, (xs, ys, _, sb, local) = self.pos, self.sems
+        there = self.out.at[pos.p, pos.c]
+        for sems, chip in ((xs, pos.px), (ys, pos.py)):
+            for j in range(2):
+                self.go(
+                    send(
+                        self.rows.at[j],
+                        there,
+                        sems.at[0, j],
+                        sems.at[1, pos.c],
+                        (pos.b, 2 * chip + j),
+                    )
+                )
+        self.go(send(self.rows.at[1 - pos.c], there, sb.at[0], sb.at[1], pos.sib))
+        self.local = pltpu.make_async_copy(self.rows.at[pos.c], there, local)
+        self.local.start()
+
+    def landed(self, sems, j, chip):
+        ref = self.out.at[chip, j]
+        send(ref, ref, sems.at[0, j], sems.at[1, j], self.pos.xn).wait_recv()
+
+    def forward(self):
+        pos, (xs, ys, fs, _, _) = self.pos, self.sems
+        self.landed(xs, 0, pos.px)
+        ref = self.out.at[pos.px, 0]
+        self.go(send(ref, ref, fs.at[0, 0], fs.at[1, 0], pos.yn))
+        self.landed(ys, 1, pos.py)
+        ref = self.out.at[pos.py, 1]
+        self.go(send(ref, ref, fs.at[0, 1], fs.at[1, 1], pos.xn))
+
+    def finish(self):
+        pos, (xs, ys, fs, sb, _) = self.pos, self.sems
+        self.landed(xs, 1, pos.px)
+        self.landed(ys, 0, pos.py)
+        self.landed(fs, 0, pos.pd)
+        self.landed(fs, 1, pos.pd)
+        ref = self.out.at[pos.p, 1 - pos.c]
+        send(ref, ref, sb.at[0], sb.at[1], pos.sib).wait_recv()
+        self.local.wait()
+
+    def drain(self):
+        for copy in self.started:
+            copy.wait_send()
+
+
+class JointGather:
+    def __init__(self, pos, parts, out, sems):
+        self.pos, self.parts, self.out = pos, parts, out
+        self.direct, self.sb, self.local_sem = sems
+        self.started = []
+
+    @staticmethod
+    def scratch(nb):
+        return [DMA((2, nb, 4)), DMA((2,)), DMA]
+
+    def start(self):
+        pos = self.pos
+        there = self.out.at[pos.b, pos.p, pos.c]
+        for d in range(pos.nb):
+            for k in range(4):
+                if d or k:
+                    chip = pos.chip(k)
+                    copy = send(
+                        self.parts.at[chip],
+                        there,
+                        self.direct.at[0, d, k],
+                        self.direct.at[1, d, k],
+                        (pos.up(d), 2 * chip + pos.c),
+                    )
+                    copy.start()
+                    self.started.append(copy)
+        self.local = pltpu.make_async_copy(self.parts.at[pos.p], there, self.local_sem)
+        self.local.start()
+
+    def sibling(self):
+        pos = self.pos
+        for d in range(pos.nb):
+            for k in range(4):
+                if d or k:
+                    ref = self.out.at[pos.down(d), pos.chip(k), pos.c]
+                    send(
+                        ref, ref, self.direct.at[0, d, k], self.direct.at[1, d, k], pos.sib
+                    ).wait_recv()
+        self.local.wait()
+        ref = self.out.at[:, :, pos.c]
+        copy = send(ref, ref, self.sb.at[0], self.sb.at[1], pos.sib)
+        copy.start()
+        self.started.append(copy)
+
+    def finish(self):
+        pos = self.pos
+        ref = self.out.at[:, :, 1 - pos.c]
+        send(ref, ref, self.sb.at[0], self.sb.at[1], pos.sib).wait_recv()
+
+    def drain(self):
+        for copy in self.started:
+            copy.wait_send()
+
+
+def gather_all(rows, joint, small, output, expand, reduce, nb):
+    def body(
+        rows_ref, joint_ref, small_ref, output_ref, expand_ref, reduce_ref,
+        rows_out, joint_out, small_out, output_out, expand_out, reduce_out,
+        *scratch,
+    ):
+        pos = Place(nb)
+        scratch = list(scratch)
+
+        def take(n):
+            got = scratch[:n]
+            del scratch[:n]
+            return got
+
+        exchange = InputExchange(pos, rows_ref, rows_out, take(5))
+        joints = JointGather(pos, joint_ref, joint_out, take(3))
+        gathers = []
+        for shard, out in (
+            (small_ref, small_out),
+            (output_ref, output_out),
+            (expand_ref, expand_out),
+            (reduce_ref, reduce_out),
+        ):
+            gathers.append(Gather(pos, shard, out, halves_of(shard.shape), take(6)))
+        local_sems = take(1)[0]
+        greet(
+            same_core(pos)
+            + [
+                pos.sib,
+                (pos.b, 2 * pos.px + 1 - pos.c),
+                (pos.b, 2 * pos.py + 1 - pos.c),
+            ]
+        )
+        exchange.start()
+        joints.start()
+        for i, gather in enumerate(gathers):
+            gather.own(local_sems.at[i])
+        for gather in gathers:
+            gather.plane(0)
+        exchange.forward()
+        for k in range(nb):
+            if k:
+                for gather in gathers:
+                    gather.plane(k)
+                for gather in gathers:
+                    gather.forward(k - 1)
+        for gather in gathers:
+            gather.forward(nb - 1)
+        joints.sibling()
+        for k in range(nb):
+            for gather in gathers:
+                gather.sibling(k)
+        exchange.finish()
+        joints.finish()
+        for gather in gathers:
+            gather.finish()
+        exchange.drain()
+        joints.drain()
+
+    def shape(shard):
+        return jax.ShapeDtypeStruct((nb, 4, 2) + shard.shape, shard.dtype)
+
+    arrays = (rows, joint, small, output, expand, reduce)
+    return pl.pallas_call(
+        body,
+        out_shape=(
+            jax.ShapeDtypeStruct((4, 2) + rows.shape[1:], rows.dtype),
+            jax.ShapeDtypeStruct((nb, 4, 2) + joint.shape[1:], joint.dtype),
+            shape(small),
+            shape(output),
+            shape(expand),
+            shape(reduce),
+        ),
+        in_specs=[ANY] * 6,
+        out_specs=(ANY,) * 6,
+        scratch_shapes=InputExchange.scratch()
+        + JointGather.scratch(nb)
+        + Gather.scratch(nb) * 4
+        + [DMA((4,))],
+        name="gather_all",
+        compiler_params=pltpu.CompilerParams(
+            collective_id=1, has_side_effects=True, vmem_limit_bytes=8 << 20
+        ),
+    )(*arrays)
+
+
+def halves_of(shape):
+    rows, columns = shape
+    if columns % 256 == 0 and columns >= 1024:
+        return (
+            (slice(None), pl.ds(0, columns // 2)),
+            (slice(None), pl.ds(columns // 2, columns // 2)),
+        )
+    if rows % 32 == 0:
+        return (
+            (pl.ds(0, rows // 2), slice(None)),
+            (pl.ds(rows // 2, rows // 2), slice(None)),
+        )
+    if columns % 256 == 0:
+        return (
+            (slice(None), pl.ds(0, columns // 2)),
+            (slice(None), pl.ds(columns // 2, columns // 2)),
+        )
+    return ((slice(None), slice(None)), None)
+
+
+def plane_exchange(parts, collective_id, name):
+    def body(parts_ref, out_ref, sems, local_sem):
+        pos = Place(1)
+        greet(plane_others(pos))
+        copies = []
+        there = out_ref.at[pos.p, pos.c]
+        for k in range(4):
+            for j in range(2):
+                chip = pos.chip(k)
+                core = pos.c if j == 0 else 1 - pos.c
+                if k or j:
+                    copies.append(
+                        send(
+                            parts_ref.at[chip, core],
+                            there,
+                            sems.at[0, 2 * k + j],
+                            sems.at[1, 2 * k + j],
+                            (pos.b, 2 * chip + core),
+                        )
+                    )
+        for copy in copies:
+            copy.start()
+        local = pltpu.make_async_copy(parts_ref.at[pos.p, pos.c], there, local_sem)
+        local.start()
+        for k in range(4):
+            for j in range(2):
+                if k or j:
+                    ref = out_ref.at[pos.chip(k), pos.c if j == 0 else 1 - pos.c]
+                    send(
+                        ref, ref, sems.at[0, 2 * k + j], sems.at[1, 2 * k + j], pos.sib
+                    ).wait_recv()
+        local.wait()
+        for copy in copies:
+            copy.wait_send()
+
+    return pl.pallas_call(
+        body,
+        out_shape=jax.ShapeDtypeStruct(parts.shape, parts.dtype),
+        in_specs=[ANY],
+        out_specs=ANY,
+        scratch_shapes=[DMA((2, 8)), DMA],
+        name=name,
+        compiler_params=pltpu.CompilerParams(
+            collective_id=collective_id, has_side_effects=True, vmem_limit_bytes=8 << 20
+        ),
+    )(parts)
+
+
+def attend(length, rows, weight, bias, heads):
+    size, _ = rows.shape
+    width = weight.shape[1] // 3
+    step = math.gcd(size, 256)
+
+    def body(length_ref, rows_ref, weight_ref, bias_ref, context_ref, qkv_ref, log_ref):
+        limit = length_ref[0]
+
+        def project(i, _):
+            at = pl.ds(pl.multiple_of(i * step, step), step)
+            qkv_ref[at, :] = (
+                jnp.dot(rows_ref[at, :], weight_ref[...], preferred_element_type=F32)
+                + bias_ref[...]
+            ).astype(BF16)
+            return 0
+
+        lax.fori_loop(0, size // step, project, 0)
+
+        def block(i, _):
+            at = pl.ds(pl.multiple_of(i * step, step), step)
+            allowed = lax.broadcasted_iota(jnp.int32, (1, size), 1) < limit
+            lanes = lax.broadcasted_iota(jnp.int32, (step, 128), 1)
+            parts, logs = [], jnp.zeros((step, 128), F32)
+            for h in range(heads):
+                query = qkv_ref[at, h * HEAD_DIM : (h + 1) * HEAD_DIM]
+                key = qkv_ref[:, width + h * HEAD_DIM : width + (h + 1) * HEAD_DIM]
+                value = qkv_ref[:, 2 * width + h * HEAD_DIM : 2 * width + (h + 1) * HEAD_DIM]
+                scores = (
+                    lax.dot_general(
+                        query, key, (((1,), (1,)), ((), ())), preferred_element_type=F32
+                    )
+                    * SCORE_SCALE
+                )
+                scores = jnp.where(allowed, scores, NEG_FILL)
+                top = jnp.max(scores, axis=-1, keepdims=True)
+                exps = jnp.exp(scores - top)
+                total = jnp.sum(exps, axis=-1, keepdims=True)
+                mixed = jnp.dot(exps.astype(BF16), value, preferred_element_type=F32)
+                parts.append(mixed / total)
+                logs = jnp.where(lanes == h, top + jnp.log(total), logs)
+            context_ref[at, :] = jnp.concatenate(parts, axis=1).astype(BF16)
+            log_ref[at, :] = logs
+            return 0
+
+        lax.fori_loop(0, size // step, block, 0)
+
+    return pl.pallas_call(
+        body,
+        out_shape=(
+            jax.ShapeDtypeStruct((size, width), BF16),
+            jax.ShapeDtypeStruct((size, 3 * width), BF16),
+            jax.ShapeDtypeStruct((size, 128), F32),
+        ),
+        in_specs=[SM, VM, VM, VM],
+        out_specs=(VM, VM, VM),
+        name="attend",
+        compiler_params=pltpu.CompilerParams(vmem_limit_bytes=48 << 20),
+    )(length, rows, weight, bias)
+
+
+def attend_back(length, rows, weight, qkv, logs, grad_context, heads):
+    size, model_width = rows.shape
+    width = weight.shape[1] // 3
+    step = math.gcd(size, 256)
+
+    def body(
+        length_ref, rows_ref, weight_ref, qkv_ref, log_ref, grad_ref,
+        grad_rows_ref, grad_weight_ref, sums_ref,
+        grad_qkv, grad_key, grad_value,
+    ):
+        limit = length_ref[0]
+        grad_key[...] = jnp.zeros_like(grad_key)
+        grad_value[...] = jnp.zeros_like(grad_value)
+
+        def block(i, _):
+            at = pl.ds(pl.multiple_of(i * step, step), step)
+            allowed = lax.broadcasted_iota(jnp.int32, (1, size), 1) < limit
+            parts = []
+            for h in range(heads):
+                query = qkv_ref[at, h * HEAD_DIM : (h + 1) * HEAD_DIM]
+                key = qkv_ref[:, width + h * HEAD_DIM : width + (h + 1) * HEAD_DIM]
+                value = qkv_ref[:, 2 * width + h * HEAD_DIM : 2 * width + (h + 1) * HEAD_DIM]
+                grad_out = grad_ref[at, h * HEAD_DIM : (h + 1) * HEAD_DIM]
+                scores = (
+                    lax.dot_general(
+                        query, key, (((1,), (1,)), ((), ())), preferred_element_type=F32
+                    )
+                    * SCORE_SCALE
+                )
+                probs = jnp.where(
+                    allowed, jnp.exp(scores - log_ref[at, h : h + 1]), 0.0
+                )
+                grad_probs = lax.dot_general(
+                    grad_out, value, (((1,), (1,)), ((), ())), preferred_element_type=F32
+                )
+                delta = jnp.sum(probs * grad_probs, axis=-1, keepdims=True)
+                grad_scores = (probs * (grad_probs - delta)).astype(BF16)
+                parts.append(
+                    jnp.dot(grad_scores, key, preferred_element_type=F32) * SCORE_SCALE
+                )
+                grad_key[h] += lax.dot_general(
+                    grad_scores, query, (((0,), (0,)), ((), ())), preferred_element_type=F32
+                )
+                grad_value[h] += lax.dot_general(
+                    probs.astype(BF16),
+                    grad_out,
+                    (((0,), (0,)), ((), ())),
+                    preferred_element_type=F32,
+                )
+            grad_qkv[at, :width] = jnp.concatenate(parts, axis=1).astype(BF16)
+            return 0
+
+        lax.fori_loop(0, size // step, block, 0)
+        grad_qkv[:, width : 2 * width] = (
+            jnp.concatenate([grad_key[h] for h in range(heads)], axis=1) * SCORE_SCALE
+        ).astype(BF16)
+        grad_qkv[:, 2 * width :] = jnp.concatenate(
+            [grad_value[h] for h in range(heads)], axis=1
+        ).astype(BF16)
+        sums_ref[...] = jnp.sum(grad_qkv[...].astype(F32), axis=0, keepdims=True)
+
+        def spread(i, _):
+            at = pl.ds(pl.multiple_of(i * step, step), step)
+            grad_rows_ref[at, :] = lax.dot_general(
+                grad_qkv[at, :],
+                weight_ref[...],
+                (((1,), (1,)), ((), ())),
+                preferred_element_type=F32,
+            ).astype(BF16)
+            return 0
+
+        lax.fori_loop(0, size // step, spread, 0)
+        grad_weight_ref[...] = lax.dot_general(
+            rows_ref[...], grad_qkv[...], (((0,), (0,)), ((), ())), preferred_element_type=F32
+        ).astype(BF16)
+
+    return pl.pallas_call(
+        body,
+        out_shape=(
+            jax.ShapeDtypeStruct((size, model_width), BF16),
+            jax.ShapeDtypeStruct((model_width, 3 * width), BF16),
+            jax.ShapeDtypeStruct((1, 3 * width), F32),
+        ),
+        in_specs=[SM, VM, VM, VM, VM, VM],
+        out_specs=(VM, VM, VM),
+        scratch_shapes=[
+            pltpu.VMEM((size, 3 * width), BF16),
+            pltpu.VMEM((heads, size, HEAD_DIM), F32),
+            pltpu.VMEM((heads, size, HEAD_DIM), F32),
+        ],
+        name="attend_back",
+        compiler_params=pltpu.CompilerParams(vmem_limit_bytes=48 << 20),
+    )(length, rows, weight, qkv, logs, grad_context)
+
+
+class Scatter:
+    def __init__(self, pos, partial, halves, bufs, sems):
+        self.pos, self.partial, self.halves = pos, partial, halves
+        (self.mine, self.theirs, self.a0, self.a1, self.bx, self.by, self.tz, self.z) = bufs
+        (self.sb, self.s0, self.s1, self.dx, self.dy, self.cx, self.cy, self.zs, self.ld) = sems
+        self.started = []
+
+    @staticmethod
+    def scratch(nb, shape, dtype, halves):
+        rows, columns = shape
+        first, second = half_shapes(shape, halves)
+        return [
+            pltpu.VMEM((nb, 4) + shape, dtype),
+            pltpu.VMEM((nb, 4) + shape, dtype),
+            pltpu.VMEM((nb,) + first, dtype),
+            pltpu.VMEM((nb,) + second, dtype),
+            pltpu.VMEM((nb,) + shape, dtype),
+            pltpu.VMEM((nb,) + shape, dtype),
+            pltpu.VMEM((nb,) + shape, dtype),
+            pltpu.VMEM((nb,) + shape, dtype),
+        ]
+
+    @staticmethod
+    def sem_scratch(nb):
+        return [DMA((2,))] + [DMA((2, nb)) for _ in range(7)] + [DMA]
+
+    def go(self, copy):
+        copy.start()
+        self.started.append(copy)
+
+    def begin(self):
+        pos = self.pos
+        self.go(
+            send(
+                self.partial.at[:, :, 1 - pos.c],
+                self.theirs,
+                self.sb.at[0],
+                self.sb.at[1],
+                pos.sib,
+            )
+        )
+        self.local = pltpu.make_async_copy(
+            self.partial.at[:, :, pos.c], self.mine, self.ld
+        )
+        self.local.start()
+
+    def joined(self):
+        self.local.wait()
+        pos = self.pos
+        send(self.theirs, self.theirs, self.sb.at[0], self.sb.at[1], pos.sib).wait_recv()
+
+    def first(self, k):
+        pos, mine = self.pos, self.mine
+        h0, h1 = self.halves
+        z = pos.up(k)
+        for j in range(4):
+            chip = pos.chip(j)
+            mine[z, chip] = (
+                mine[z, chip].astype(F32) + self.theirs[z, chip].astype(F32)
+            ).astype(mine.dtype)
+        there = mine.at[z, pos.pd]
+        self.go(send(there.at[h0], self.a0.at[k], self.s0.at[0, k], self.s0.at[1, k], pos.xn))
+        if h1 is not None:
+            self.go(
+                send(there.at[h1], self.a1.at[k], self.s1.at[0, k], self.s1.at[1, k], pos.yn)
+            )
+        self.go(
+            send(
+                mine.at[z, pos.px].at[h0],
+                self.bx.at[k].at[h0],
+                self.dx.at[0, k],
+                self.dx.at[1, k],
+                pos.xn,
+            )
+        )
+        if h1 is not None:
+            self.go(
+                send(
+                    mine.at[z, pos.py].at[h1],
+                    self.by.at[k].at[h1],
+                    self.dy.at[0, k],
+                    self.dy.at[1, k],
+                    pos.yn,
+                )
+            )
+
+    def landed(self, ref, sems, k):
+        send(ref, ref, sems.at[0, k], sems.at[1, k], self.pos.xn).wait_recv()
+
+    def second(self, k):
+        pos, mine = self.pos, self.mine
+        h0, h1 = self.halves
+        z = pos.up(k)
+        self.landed(self.a0.at[k], self.s0, k)
+        ref = mine.at[z, pos.py]
+        ref[h0] = (ref[h0].astype(F32) + self.a0[k].astype(F32)).astype(mine.dtype)
+        self.go(
+            send(
+                ref.at[h0], self.by.at[k].at[h0], self.cy.at[0, k], self.cy.at[1, k], pos.yn
+            )
+        )
+        if h1 is not None:
+            self.landed(self.a1.at[k], self.s1, k)
+            ref = mine.at[z, pos.px]
+            ref[h1] = (ref[h1].astype(F32) + self.a1[k].astype(F32)).astype(mine.dtype)
+            self.go(
+                send(
+                    ref.at[h1], self.bx.at[k].at[h1], self.cx.at[0, k], self.cx.at[1, k], pos.xn
+                )
+            )
+
+    def third(self, k, total):
+        pos = self.pos
+        h0, h1 = self.halves
+        z = pos.up(k)
+        self.landed(self.bx.at[k].at[h0], self.dx, k)
+        self.landed(self.by.at[k].at[h0], self.cy, k)
+        if h1 is not None:
+            self.landed(self.by.at[k].at[h1], self.dy, k)
+            self.landed(self.bx.at[k].at[h1], self.cx, k)
+        value = (
+            self.mine[z, pos.p].astype(F32)
+            + self.bx[k].astype(F32)
+            + self.by[k].astype(F32)
+        )
+        if k:
+            self.tz[k] = value.astype(self.tz.dtype)
+            self.go(
+                send(
+                    self.tz.at[k],
+                    self.z.at[k],
+                    self.zs.at[0, k],
+                    self.zs.at[1, k],
+                    (pos.up(k), pos.s),
+                )
+            )
+        else:
+            total[...] = value
+
+    def last(self, total):
+        pos = self.pos
+        value = total[...]
+        for k in range(1, pos.nb):
+            self.landed(self.z.at[k], self.zs, k)
+            value = value + self.z[k].astype(F32)
+        total[...] = value
+
+    def drain(self):
+        for copy in self.started:
+            copy.wait_send()
+
+
+def half_shapes(shape, halves):
+    def cut(half):
+        return tuple(n if h == slice(None) else h.size for n, h in zip(shape, half))
+
+    first = cut(halves[0])
+    return first, (first if halves[1] is None else cut(halves[1]))
+
+
+class RowScatter:
+    def __init__(self, pos, partial, out, bufs, sems):
+        self.pos, self.partial, self.out = pos, partial, out
+        self.mine, self.a0, self.a1, self.bx, self.by, self.far = bufs
+        self.sm, self.ld = sems
+        self.started = []
+
+    @staticmethod
+    def scratch(rows, columns):
+        return [
+            pltpu.VMEM((4, 2, rows, columns), BF16),
+            pltpu.VMEM((rows, columns), BF16),
+            pltpu.VMEM((rows, columns), BF16),
+            pltpu.VMEM((2, rows, columns), BF16),
+            pltpu.VMEM((2, rows, columns), BF16),
+            pltpu.VMEM((rows, columns), F32),
+            DMA((2, 7)),
+            DMA,
+        ]
+
+    def go(self, i, src, dst, device):
+        copy = send(src, dst, self.sm.at[0, i], self.sm.at[1, i], device)
+        copy.start()
+        self.started.append(copy)
+
+    def landed(self, i, ref):
+        send(ref, ref, self.sm.at[0, i], self.sm.at[1, i], self.pos.xn).wait_recv()
+
+    def begin(self):
+        self.local = pltpu.make_async_copy(self.partial, self.mine, self.ld)
+        self.local.start()
+
+    def first(self):
+        pos, mine = self.pos, self.mine
+        self.local.wait()
+        self.go(0, mine.at[pos.pd, 0], self.a0, pos.xn)
+        self.go(1, mine.at[pos.pd, 1], self.a1, pos.yn)
+        self.go(2, mine.at[pos.px, 0], self.bx.at[0], pos.xn)
+        self.go(3, mine.at[pos.py, 1], self.by.at[1], pos.yn)
+
+    def second(self):
+        pos, mine = self.pos, self.mine
+        self.landed(0, self.a0)
+        mine[pos.py, 0] = (mine[pos.py, 0].astype(F32) + self.a0[...].astype(F32)).astype(BF16)
+        self.go(4, mine.at[pos.py, 0], self.by.at[0], pos.yn)
+        self.landed(1, self.a1)
+        mine[pos.px, 1] = (mine[pos.px, 1].astype(F32) + self.a1[...].astype(F32)).astype(BF16)
+        self.go(5, mine.at[pos.px, 1], self.bx.at[1], pos.xn)
+
+    def third(self):
+        pos = self.pos
+        self.landed(2, self.bx.at[0])
+        self.landed(3, self.by.at[1])
+        self.landed(4, self.by.at[0])
+        self.landed(5, self.bx.at[1])
+
+        def total(core):
+            return (
+                self.mine[pos.p, core].astype(F32)
+                + self.bx[core].astype(F32)
+                + self.by[core].astype(F32)
+            )
+
+        self.far[...] = total(1 - pos.c)
+        self.go(6, self.far, self.out.at[pos.c], pos.sib)
+        self.out[pos.c] = total(pos.c)
+
+    def last(self):
+        pos = self.pos
+        self.landed(6, self.out.at[1 - pos.c])
+        for copy in self.started:
+            copy.wait_send()
+
+
+class JointScatter:
+    def __init__(self, pos, partial, bufs, sems):
+        self.pos, self.partial = pos, partial
+        self.mine, self.theirs, self.got = bufs
+        self.sb, self.direct, self.ld = sems
+        self.started = []
+
+    @staticmethod
+    def scratch(nb, shape):
+        return [pltpu.VMEM((nb, 4) + shape, BF16) for _ in range(3)]
+
+    @staticmethod
+    def sem_scratch(nb):
+        return [DMA((2,)), DMA((2, nb, 4)), DMA]
+
+    def begin(self):
+        pos = self.pos
+        copy = send(
+            self.partial.at[:, :, 1 - pos.c], self.theirs, self.sb.at[0], self.sb.at[1], pos.sib
+        )
+        copy.start()
+        self.started.append(copy)
+        self.local = pltpu.make_async_copy(
+            self.partial.at[:, :, pos.c], self.mine, self.ld
+        )
+        self.local.start()
+
+    def first(self):
+        pos, mine = self.pos, self.mine
+        self.local.wait()
+        send(self.theirs, self.theirs, self.sb.at[0], self.sb.at[1], pos.sib).wait_recv()
+        mine[...] = (mine[...].astype(F32) + self.theirs[...].astype(F32)).astype(BF16)
+        for d in range(pos.nb):
+            for k in range(4):
+                if d or k:
+                    chip = pos.chip(k)
+                    copy = send(
+                        mine.at[pos.up(d), chip],
+                        self.got.at[d, k],
+                        self.direct.at[0, d, k],
+                        self.direct.at[1, d, k],
+                        (pos.up(d), 2 * chip + pos.c),
+                    )
+                    copy.start()
+                    self.started.append(copy)
+
+    def last(self, out):
+        pos = self.pos
+        for k in range(4):
+            value = None
+            for d in range(pos.nb):
+                if d or k:
+                    ref = self.got.at[d, k]
+                    send(
+                        ref, ref, self.direct.at[0, d, k], self.direct.at[1, d, k], pos.sib
+                    ).wait_recv()
+                    term = self.got[d, k].astype(F32)
+                else:
+                    term = self.mine[pos.b, pos.p].astype(F32)
+                value = term if value is None else value + term
+            out[pos.chip(k)] = value
+        for copy in self.started:
+            copy.wait_send()
+
+
+def scatter_all(grad_rows, joint, small, output, expand, reduce, nb):
+    arrays = (small, output, expand, reduce)
+    shapes = [a.shape[3:] for a in arrays]
+    row_shape = grad_rows.shape[2:]
+    joint_shape = joint.shape[3:]
+
+    def body(
+        rows_ref, joint_ref, small_ref, output_ref, expand_ref, reduce_ref,
+        rows_out, joint_out, small_out, output_out, expand_out, reduce_out,
+        *scratch,
+    ):
+        pos = Place(nb)
+        scratch = list(scratch)
+
+        def take(n):
+            got = scratch[:n]
+            del scratch[:n]
+            return got
+
+        rows = RowScatter(pos, rows_ref, rows_out, take(6), take(2))
+        joints = JointScatter(pos, joint_ref, take(3), take(3))
+        outs = (small_out, output_out, expand_out, reduce_out)
+        scatters = [
+            Scatter(pos, ref, halves_of(ref.shape[3:]), take(8), take(9))
+            for ref in (small_ref, output_ref, expand_ref, reduce_ref)
+        ]
+        greet(same_core(pos) + [pos.sib])
+        rows.begin()
+        for scatter in scatters:
+            scatter.begin()
+        joints.begin()
+        rows.first()
+        order = [k for k in range(1, nb)] + [0]
+        for scatter in scatters:
+            scatter.joined()
+        for k in order:
+            for scatter in scatters:
+                scatter.first(k)
+            if k == order[0]:
+                joints.first()
+                rows.second()
+        for k in order:
+            for scatter in scatters:
+                scatter.second(k)
+        rows.third()
+        for k in order:
+            for scatter, out in zip(scatters, outs):
+                scatter.third(k, out)
+        joints.last(joint_out)
+        for scatter, out in zip(scatters, outs):
+            scatter.last(out)
+            scatter.drain()
+        rows.last()
+
+    scratch = RowScatter.scratch(*row_shape) + JointScatter.scratch(nb, joint_shape)
+    scratch += JointScatter.sem_scratch(nb)
+    for array, shape in zip(arrays, shapes):
+        scratch += Scatter.scratch(nb, shape, array.dtype, halves_of(shape))
+        scratch += Scatter.sem_scratch(nb)
+    return pl.pallas_call(
+        body,
+        out_shape=(
+            jax.ShapeDtypeStruct((2,) + row_shape, F32),
+            jax.ShapeDtypeStruct((4,) + joint_shape, F32),
+        )
+        + tuple(jax.ShapeDtypeStruct(shape, F32) for shape in shapes),
+        in_specs=[ANY] * 6,
+        out_specs=(VM,) * 6,
+        scratch_shapes=scratch,
+        name="scatter_all",
+        compiler_params=pltpu.CompilerParams(
+            collective_id=4, has_side_effects=True, vmem_limit_bytes=VMEM_LIMIT
+        ),
+    )(grad_rows, joint, small, output, expand, reduce)
+
+
+def plane_on_device(
+    inputs,
+    cotangent,
+    lengths,
+    joint_weight,
+    output_weight,
+    vectors,
+    expand_weight,
+    expand_bias,
+    reduce_weight,
+):
+    nb = lax.axis_size("batch")
+    seq_count, row_count, model_width = inputs.shape
+    tokens = seq_count * row_count
+    hidden_width = expand_weight.shape[1]
+    place = lax.axis_index("seq")
+    core, chip = place % 2, place // 2
+    width = model_width // 4
+    heads = width // HEAD_DIM
+    vec = vectors.shape[1]
+    per_row = expand_bias.shape[0] // 8
+    owners = 8 * nb
+
+    flat_inputs = inputs.reshape(tokens, model_width)
+    joint_parts = joint_weight.reshape(-1, 3, 4, width).transpose(2, 0, 1, 3)
+    joint_parts = joint_parts.reshape(4, -1, 3 * width)
+    small = jnp.concatenate(
+        [
+            vectors.astype(F32),
+            expand_bias.reshape(8, per_row).astype(F32),
+            jnp.zeros((8, 128 - vec - per_row), F32),
+        ],
+        axis=1,
+    )
+    rows_all, joint_all, small_all, output_all, expand_all, reduce_all = gather_all(
+        inputs.astype(BF16), joint_parts, small, output_weight, expand_weight, reduce_weight, nb
+    )
+    rows_all = rows_all.reshape(8 * row_count, model_width)
+    joint_all = joint_all.reshape(model_width, 3 * width)
+    full_output = output_all.reshape(model_width, model_width)
+    full_expand = expand_all.reshape(model_width, hidden_width)
+    full_reduce = reduce_all.reshape(hidden_width, model_width)
+    small_all = small_all.reshape(owners, 8, 128)
+    vector_rows = small_all[:, :, :vec].transpose(1, 0, 2).reshape(8, model_width)
+    full_bias = small_all[:, :, vec : vec + per_row].reshape(hidden_width)
+
+    own_bias = lax.dynamic_slice_in_dim(vector_rows[2:4], chip * width, width, 1)
+    bias = jnp.concatenate([own_bias[0], jnp.zeros((width,), F32), own_bias[1]])[None]
+    length = lax.dynamic_slice_in_dim(lengths, core, 1)
+    context, qkv, logs = attend(length, rows_all, joint_all, bias, heads)
+    mixed = plane_exchange(context.reshape(4, 2, row_count, width), 2, "context_exchange")
+    context_low = mixed.transpose(1, 2, 0, 3).reshape(tokens, model_width)
+
+    branch = jnp.dot(context_low, full_output, preferred_element_type=F32) + vector_rows[4]
+    first, first_normed, first_inverse = layer_norm(
+        flat_inputs + branch, vector_rows[0], vector_rows[1]
+    )
+    first_low = first.astype(BF16)
+    before_gelu = jnp.dot(first_low, full_expand, preferred_element_type=F32) + full_bias
+    hidden_low = gelu_value(before_gelu).astype(BF16)
+    feed = jnp.dot(hidden_low, full_reduce, preferred_element_type=F32) + vector_rows[7]
+    result, second_normed, second_inverse = layer_norm(first + feed, vector_rows[5], vector_rows[6])
+
+    own_places = place * row_count + jnp.arange(row_count, dtype=jnp.int32)
+    row_mask = (own_places[None, :] < lengths[:, None]).reshape(tokens, 1).astype(F32)
+    grad_res = cotangent.reshape(tokens, model_width) * row_mask
+    grad_second, grad_gain_two, grad_shift_two = norm_back(
+        grad_res, second_normed, second_inverse, vector_rows[5]
+    )
+    grad_feed_low = grad_second.astype(BF16)
+    grad_reduce = jnp.dot(hidden_low.T, grad_feed_low, preferred_element_type=F32)
+    grad_hidden = jnp.dot(
+        grad_feed_low, full_reduce.T, preferred_element_type=F32
+    ) * gelu_slope(before_gelu)
+    grad_hidden_low = grad_hidden.astype(BF16)
+    grad_expand = jnp.dot(first_low.T, grad_hidden_low, preferred_element_type=F32)
+    grad_bias = jnp.sum(grad_hidden_low.astype(F32), axis=0)
+    grad_first = grad_second + jnp.dot(
+        grad_hidden_low, full_expand.T, preferred_element_type=F32
+    )
+    grad_resid, grad_gain_one, grad_shift_one = norm_back(
+        grad_first, first_normed, first_inverse, vector_rows[0]
+    )
+    grad_branch_low = grad_resid.astype(BF16)
+    grad_output = jnp.dot(context_low.T, grad_branch_low, preferred_element_type=F32)
+    grad_context_low = jnp.dot(
+        grad_branch_low, full_output.T, preferred_element_type=F32
+    ).astype(BF16)
+
+    parts = grad_context_low.reshape(seq_count, row_count, 4, width).transpose(2, 0, 1, 3)
+    grad_context = plane_exchange(parts, 3, "gradient_exchange").reshape(8 * row_count, width)
+    grad_rows, grad_joint, sums = attend_back(
+        length, rows_all, joint_all, qkv, logs, grad_context, heads
+    )
+
+    def spread(own):
+        return lax.dynamic_update_slice_in_dim(
+            jnp.zeros((model_width,), F32), own, chip * width, 0
+        )
+
+    grad_vectors = jnp.stack(
+        [
+            grad_gain_one,
+            grad_shift_one,
+            spread(sums[0, :width]),
+            spread(sums[0, 2 * width :]),
+            jnp.sum(grad_branch_low.astype(F32), axis=0),
+            grad_gain_two,
+            grad_shift_two,
+            jnp.sum(grad_feed_low.astype(F32), axis=0),
+        ]
+    )
+    grad_small = jnp.concatenate(
+        [
+            grad_vectors.reshape(8, owners, vec).transpose(1, 0, 2),
+            grad_bias.reshape(owners, 8, per_row),
+            jnp.zeros((owners, 8, 128 - vec - per_row), F32),
+        ],
+        axis=2,
+    )
+
+    def split(partial):
+        return partial.reshape((nb, 4, 2, partial.shape[0] // owners) + partial.shape[1:])
+
+    rows_sum, joint_sum, small_sum, output_sum, expand_sum, reduce_sum = scatter_all(
+        grad_rows.reshape(4, 2, row_count, model_width),
+        split(grad_joint),
+        grad_small.reshape(nb, 4, 2, 8, 128),
+        split(grad_output.astype(BF16)),
+        split(grad_expand.astype(BF16)),
+        split(grad_reduce.astype(BF16)),
+        nb,
+    )
+    joint_sum = joint_sum.reshape(4, -1, 3, width).transpose(1, 2, 0, 3)
+    return (
+        result.reshape(seq_count, row_count, model_width),
+        grad_resid.reshape(seq_count, row_count, model_width) + rows_sum,
+        joint_sum.reshape(-1, 3 * model_width),
+        output_sum,
+        small_sum[:, :vec],
+        expand_sum,
+        small_sum[:, vec : vec + per_row].reshape(-1),
+        reduce_sum,
+    )
+
+
+def plane_fits(mesh, inputs, expand_bias, expand_weight):
+    return (
+        mesh.shape["seq"] == 8
+        and inputs[0] == 2 * mesh.shape["batch"]
+        and HEADS % 4 == 0
+        and inputs[2] == HEADS * HEAD_DIM
+        and inputs[1] % (8 * 16) == 0
+        and expand_weight[0] % (8 * mesh.shape["seq"] * mesh.shape["batch"]) == 0
+        and expand_bias[0] % (8 * mesh.shape["seq"] * mesh.shape["batch"]) == 0
+        and (expand_weight[0] + expand_bias[0] // 8) <= 128 * mesh.shape["seq"] * mesh.shape["batch"]
+    )
+
+
 def solution(mesh):
-    return jax.shard_map(
-        on_device,
-        mesh=mesh,
-        in_specs=(
-            P("batch", "seq", None),
-            P("batch", "seq", None),
-            P("batch"),
-            P(("batch", "seq"), None),
-            P(("batch", "seq"), None),
-            P(None, ("batch", "seq")),
-            P(("batch", "seq"), None),
-            P(("batch", "seq")),
-            P(("batch", "seq"), None),
-        ),
-        out_specs=(
-            P("batch", "seq", None),
-            P("batch", "seq", None),
-            P(("batch", "seq"), None),
-            P(("batch", "seq"), None),
-            P(None, ("batch", "seq")),
-            P(("batch", "seq"), None),
-            P(("batch", "seq")),
-            P(("batch", "seq"), None),
-        ),
-        check_vma=False,
-    )
+    def program(*args):
+        fits = plane_fits(mesh, args[0].shape, args[7].shape, args[6].shape)
+        return jax.shard_map(
+            plane_on_device if fits else general_on_device,
+            mesh=mesh,
+            in_specs=(
+                P("batch", "seq", None),
+                P("batch", "seq", None),
+                P("batch"),
+                P(("batch", "seq"), None),
+                P(("batch", "seq"), None),
+                P(None, ("batch", "seq")),
+                P(("batch", "seq"), None),
+                P(("batch", "seq")),
+                P(("batch", "seq"), None),
+            ),
+            out_specs=(
+                P("batch", "seq", None),
+                P("batch", "seq", None),
+                P(("batch", "seq"), None),
+                P(("batch", "seq"), None),
+                P(None, ("batch", "seq")),
+                P(("batch", "seq"), None),
+                P(("batch", "seq")),
+                P(("batch", "seq"), None),
+            ),
+            check_vma=False,
+        )(*args)
+
+    return program

time: 937 us -> 301 us (0.32)
  waiting for transfers between devices: 555 us -> 0 us
  Pallas kernels: 0 us -> 213 us
  blocking collectives: 140 us -> 0 us
  matrix products: 108 us -> 30.7 us
  local copies, waits for them, and re-layouts: 76 us -> 34.4 us
  other arithmetic: 39 us -> 15.9 us
  between operations: 14.8 us -> 1.36 us
    reduce_scatter x3 -> x0, waiting for transfers between devices: 242 us -> none  [the longest x1 141 us: on_device(): lax.psum_scatter(grad_reduce_local, ('batch', 'seq'), scatter_dimension=0...]
    pallas_call x0 -> x6, Pallas kernels: none -> 213 us  [the longest x1 91.5 us: scatter_all(): pl.pallas_call(body, out_shape=(jax.ShapeDtypeStruct((2,) + row_shape, F3...]
    all_gather x8 -> x0, waiting for transfers between devices: 185 us -> none  [the longest x1 64.5 us: gather_attention(): lax.all_gather(joint_weight, ('batch', 'seq'), axis=0, tiled=True)]
    unnamed x13 -> x0, waiting for transfers between devices: 128 us -> none
    unnamed x2 -> x0, blocking collectives: 77.4 us -> none
    dot_general x40 -> x9, matrix products: 108 us -> 30.7 us  [the longest x1 7.38 us: plane_on_device(): jnp.dot(grad_feed_low, full_reduce.T, preferred_element_type=F32)]
    all_gather x3 -> x0, blocking collectives: 62.9 us -> none  [the longest x1 42.5 us: gather_attention(): lax.all_gather(vectors, ('batch', 'seq'), axis=1, tiled=True)]
    dynamic_slice x16 -> x1, local copies, waits for them, and re-layouts: 31.8 us -> 0.59 us  [plane_on_device(): length = lax.dynamic_slice_in_dim(lengths, core, 1)]
  transfers between devices with their start and end apart: 12 -> 0, of which waited for: 6 -> 0; matrix products, arithmetic and copies ran while one was open for 22% -> 0% of each run, Pallas kernels for 0% -> 0%
where the time goes in v1:
time: 301 us; the launch traced here: 295 us
  Pallas kernels  213 us (71%)
  local copies, waits for them, and re-layouts  34.4 us (11%)
  matrix products  30.7 us (10%)
  other arithmetic  15.9 us (5%)
    pallas_call x1, Pallas kernels, scatter_all(): pl.pallas_call(body, out_shape=(jax.ShapeDtypeStruct((2,) + row_shape, F3...  91.5 us
    pallas_call x1, Pallas kernels, gather_all(): pl.pallas_call(body, out_shape=(jax.ShapeDtypeStruct((4, 2) + rows.shape[...  74.5 us
    pallas_call x1, Pallas kernels, attend_back(): pl.pallas_call(body, out_shape=(jax.ShapeDtypeStruct((size, model_width),...  18.9 us
    unnamed x108, local copies, waits for them, and re-layouts  18.5 us
    pallas_call x2, Pallas kernels, plane_exchange(): pl.pallas_call(body, out_shape=jax.ShapeDtypeStruct(parts.shape, parts.dt...  18.4 us
    pallas_call x1, Pallas kernels, attend(): pl.pallas_call(body, out_shape=(jax.ShapeDtypeStruct((size, width), BF16)...  9.65 us
    dot_general x1, matrix products, plane_on_device(): jnp.dot(grad_feed_low, full_reduce.T, preferred_element_type=F32)  7.38 us

profile of v1, /device:TPU:0, one launch (start us, length us, event | category | flops | bytes accessed | tf_op | source)
XLA Modules:
  0.0 295.4 jit_solution(15239701247526402259)
XLA Ops:
  7.8 74.5 %gather_all.1 = (bf16[4,2,128,768]{3,2,1,0:T(8,128)(2,1)S(1)}, bf16[4,4,2,24,576]{4,3,2,1,0:T(8,128)(2,1)S(1)}, f32[4,4,2,8,128]{4,3,2,1,0:T(8,128)S(1)}, bf16[4...) custom-call(bf16[2,128,768]{2,1,0:T(8,128)(2,1)S(1)} %convert_elemen, ...), custom_call_target="tpu_custom_call" | custom-call | tf_op jit(solution)/shard_map/gather_all/pallas_call | solution.py:649
  83.2 2.1 copy-done.13
  85.4 2.2 copy-done.14
  92.0 9.6 %attend.1 = (bf16[1024,192]{1,0:T(8,128)(2,1)S(1)}, bf16[1024,576]{1,0:T(8,128)(2,1)S(1)}, f32[1024,128]{1,0:T(8,128)S(1)}) custom-call(s32[1]{0:T(128)} %dynamic_slice.6.length_ref, bf16[1024,768]{1,0:T(8,128)(2,1)S(1)} %bitcast.69, bf16[768,576]{1,0:T(8,128)(2,1)S(1)} %bitcast.73, f32[1,576]{1,0:T(1,128)S(1)} %broadcast_in_dim.10.bias_ref), custom_call_target="tpu_custom_call" | custom-call | tf_op jit(solution)/shard_map/attend/pallas_call | solution.py:786
  103.5 9.2 %context_exchange.1 = bf16[4,2,128,192]{3,2,1,0:T(8,128)(2,1)S(1)} custom-call(bf16[4,2,128,192]{3,2,1,0:T(8,128)(2,1)S(1)} %bitcast.80), custom_call_target="tpu_custom_call" | custom-call | tf_op jit(solution)/shard_map/context_exchange/pallas_call | solution.py:727
  113.8 1.8 fusion.22
  117.5 6.0 %multiply_convert_fusion = (bf16[256,3072]{1,0:T(8,128)(2,1)S(1)}, f32[256,3072]{1,0:T(8,128)}) fusion(f32[3072]{0:T(1024)} %add.119, bf16[768,3072]{1,0:T(8,128)(2,1)} %bitcast.83, f32[256,768]{1,0:T(8,128)S(1)} %get-tuple-element.70, f32[768]{0:T(1024)S(1)} %add.116, f32[768]{0:T(1024)S(1)} %mul.159, f32[256]{0:T(256)S(1)} %add_rsqrt_fusion.1, ...), kind=kOutput, calls=%fused_computation.11 | convolution fusion | flops 1213661184 | bytes 10244096 | tf_op jit(solution)/shard_map/dot_general | solution.py:1328
  123.6 2.1 fusion.23
  125.7 1.3 compare_convert_fusion
  129.3 1.6 multiply_reduce_fusion
  131.5 1.5 multiply_reduce_fusion.7
  133.6 1.4 add.128
  135.0 2.7 convert_reduce_fusion.1
  137.7 7.4 %convert_reduce_fusion = (f32[3072]{0:T(1024)}, bf16[256,3072]{1,0:T(8,128)(2,1)S(1)}) fusion(f32[256,3072]{1,0:T(8,128)} %get-tuple-element.72, bf16[3072,768]{1,0:T(8,128)(2,1)} %bitcast.87, f32[256,768]{1,0:T(8,128)S(1)} %get-tuple-element.53), kind=kOutput, calls=%fused_computation.10 | convolution fusion | flops 1217590272 | bytes 10235904 | tf_op jit(solution)/shard_map/dot_general | solution.py:1341
  145.1 2.2 multiply_reduce_fusion.1
  150.3 1.5 reshape.243
  152.0 9.3 %gradient_exchange.1 = bf16[4,2,128,192]{3,2,1,0:T(8,128)(2,1)S(1)} custom-call(bf16[4,2,128,192]{3,2,1,0:T(8,128)(2,1)S(1)} %bitcast.77), custom_call_target="tpu_custom_call" | custom-call | tf_op jit(solution)/shard_map/gradient_exchange/pallas_call | solution.py:727
  161.3 1.3 copy-done.6
  162.6 18.9 %attend_back.1 = (bf16[1024,768]{1,0:T(8,128)(2,1)S(1)}, bf16[768,576]{1,0:T(8,128)(2,1)S(1)}, f32[1,576]{1,0:T(1,128)S(1)}) custom-call(s32[1]{0:T(128)} %dynamic_slice.6.length_ref, bf16[1024,768]{1,0:T(8,128)(2,1)} %bitcast.70, bf16[768,576]{1,0:T(8,128)(2,1)S(1)} %bitcast.74, bf16[1024,576]{1,0:T(8,128)(2,1)S(1)} %copy-done.6, ...), custom_call_target="tpu_custom_call" | custom-call | tf_op jit(solution)/shard_map/attend_back/pallas_call | solution.py:876
  186.2 2.6 convolution_convert_fusion.2
  188.8 3.7 %convolution_convert_fusion.1 = bf16[768,3072]{1,0:T(8,128)(2,1)} fusion(bf16[256,3072]{1,0:T(8,128)(2,1)S(1)} %copy-done.24, f32[256,768]{1,0:T(8,128)S(1)} %get-tuple-element.70, f32[768]{0:T(1024)S(1)} %add.116, f32[768]{0:T(1024)S(1)} %mul.159, f32[256]{0:T(256)S(1)} %copy-done.36, f32[256]{0:T(256)S(1)} %broadcast_multiply_fusion.4), kind=kOutput, calls=%fused_computation.1 | convolution fusion | flops 1211301888 | bytes 7086080 | tf_op jit(solution)/shard_map/dot_general | solution.py:1345
  192.5 3.6 %convolution_convert_fusion = bf16[3072,768]{1,0:T(8,128)(2,1)} fusion(bf16[256,3072]{1,0:T(8,128)(2,1)S(1)} %copy-done.19, f32[256,768]{1,0:T(8,128)S(1)} %copy-done.22), kind=kOutput, calls=%fused_computation | convolution fusion | flops 1210515456 | bytes 7077888 | tf_op jit(solution)/shard_map/dot_general | solution.py:1340
  196.1 91.5 %scatter_all.1 = (f32[2,128,768]{2,1,0:T(8,128)}, f32[4,24,576]{2,1,0:T(8,128)}, f32[8,128]{1,0:T(8,128)}, f32[24,768]{1,0:T(8,128)}, f32[24,3072]{1,0:T(8,128)}, /*index=5*/f32[96,768]{1,0:T(8,128)}) custom-call(bf16[4,2,128,768]{3,2,1,0:T(8,128)(2,1)} %bitcast.78, bf16[4,4,2,24,576]{4,3,2,1,0:T(8,128)(2,1)} %bitcast.79, ...), custom_call_target="tpu_custom_call" | custom-call | tf_op jit(solution)/shard_map/scatter_all/pallas_call | solution.py:1253
  287.7 2.2 add.135
  (169 shorter events, 33.7 us)
Async XLA Ops:
  0.6 89.2 %copy-start.43 = (s32[2]{0:T(128)S(1)}, s32[2]{0:T(128)}, u32[]{:S(2)}) copy-start(s32[2]{0:T(128)} %param.11) | copy-start | bytes 28
  87.5 28.1 %copy-start = (bf16[4,2,128,768]{3,2,1,0:T(8,128)(2,1)}, bf16[4,2,128,768]{3,2,1,0:T(8,128)(2,1)S(1)}, u32[]{:S(2)}) copy-start(bf16[4,2,128,768]{3,2,1,0:T(8,128)(2,1)S(1)} %get-tuple-element.26) | copy-start | bytes 4718596
  117.2 6.3 %slice-start.2 = ((s8[4718592]{0:T(1024)(128)(4,1)}), s8[4194304]{0:T(1024)(128)(4,1)S(1)}, s32[]{:S(2)}) async-start(s8[4718592]{0:T(1024)(128)(4,1)} %bitcast.88), calls=%async_computation.2 | async-start | bytes 8388608
  117.5 6.0 %copy-start.34 = (f32[256]{0:T(256)}, f32[256]{0:T(256)S(1)}, u32[]{:S(2)}) copy-start(f32[256]{0:T(256)S(1)} %add_rsqrt_fusion.1) | copy-start | bytes 3076
  117.5 6.0 %slice-start.3 = ((s8[4718592]{0:T(1024)(128)(4,1)}), s8[524288]{0:T(1024)(128)(4,1)S(1)}, s32[]{:S(2)}) async-start(s8[4718592]{0:T(1024)(128)(4,1)} %bitcast.88), calls=%async_computation.3 | async-start | bytes 1048576
  134.9 10.1 %slice-start = ((s8[4718592]{0:T(1024)(128)(4,1)}), s8[4194304]{0:T(1024)(128)(4,1)S(1)}, s32[]{:S(2)}) async-start(s8[4718592]{0:T(1024)(128)(4,1)} %bitcast.84), calls=%async_computation | async-start | bytes 8388608
  137.7 7.4 %copy-start.21 = (f32[256,768]{1,0:T(8,128)}, f32[256,768]{1,0:T(8,128)S(1)}, u32[]{:S(2)}) copy-start(f32[256,768]{1,0:T(8,128)S(1)} %get-tuple-element.53) | copy-start | bytes 2359300
  137.7 7.4 %slice-start.1 = ((s8[4718592]{0:T(1024)(128)(4,1)}), s8[524288]{0:T(1024)(128)(4,1)S(1)}, s32[]{:S(2)}) async-start(s8[4718592]{0:T(1024)(128)(4,1)} %bitcast.84), calls=%async_computation.1 | async-start | bytes 1048576
  137.7 7.4 %copy-start.35 = (f32[256]{0:T(256)S(1)}, f32[256]{0:T(256)}, u32[]{:S(2)}) copy-start(f32[256]{0:T(256)} %copy-done.34) | copy-start | bytes 3076
  148.2 13.1 %copy-start.3 = (bf16[4,4,2,24,576]{4,3,2,1,0:T(8,128)(2,1)S(1)}, bf16[4,4,2,24,576]{4,3,2,1,0:T(8,128)(2,1)}, u32[]{:S(2)}) copy-start(bf16[4,4,2,24,576]{4,3,2,1,0:T(8,128)(2,1)} %copy-done.1) | copy-start | bytes 2654212
  148.2 13.1 %copy-start.9 = (f32[1024,128]{1,0:T(8,128)S(1)}, f32[1024,128]{1,0:T(8,128)}, u32[]{:S(2)}) copy-start(f32[1024,128]{1,0:T(8,128)} %copy-done.8) | copy-start | bytes 1572868
  151.9 31.8 %copy-start.37 = (f32[3072]{0:T(1024)S(1)}, f32[3072]{0:T(1024)}, u32[]{:S(2)}) copy-start(f32[3072]{0:T(1024)} %get-tuple-element.76) | copy-start | bytes 36868
  151.9 31.9 %copy-start.40 = (f32[768]{0:T(1024)S(1)}, f32[768]{0:T(1024)}, u32[]{:S(2)}) copy-start(f32[768]{0:T(1024)} %get-tuple-element.46) | copy-start | bytes 9220
  151.9 32.0 %copy-start.39 = (f32[768]{0:T(1024)S(1)}, f32[768]{0:T(1024)}, u32[]{:S(2)}) copy-start(f32[768]{0:T(1024)} %get-tuple-element.51) | copy-start | bytes 9220
  152.0 32.9 %copy-start.32 = (f32[768]{0:T(1024)S(1)}, f32[768]{0:T(1024)}, u32[]{:S(2)}) copy-start(f32[768]{0:T(1024)} %get-tuple-element.54) | copy-start | bytes 9220
  152.0 33.0 %copy-start.29 = (f32[768]{0:T(1024)S(1)}, f32[768]{0:T(1024)}, u32[]{:S(2)}) copy-start(f32[768]{0:T(1024)} %get-tuple-element.44) | copy-start | bytes 9220
  152.0 33.1 %copy-start.30 = (f32[768]{0:T(1024)S(1)}, f32[768]{0:T(1024)}, u32[]{:S(2)}) copy-start(f32[768]{0:T(1024)} %get-tuple-element.49) | copy-start | bytes 9220
  152.0 33.2 %copy-start.31 = (f32[768]{0:T(1024)S(1)}, f32[768]{0:T(1024)}, u32[]{:S(2)}) copy-start(f32[768]{0:T(1024)} %get-tuple-element.52) | copy-start | bytes 9220
  161.3 24.1 %copy-start.42 = (f32[128]{0:T(128)S(1)}, f32[128]{0:T(128)}, u32[]{:S(2)}) copy-start(f32[128]{0:T(128)} %copy-done.41) | copy-start | bytes 1540
  162.6 23.6 %copy-start.20 = (bf16[2,128,4,192]{1,0,3,2:T(2,128)(2,1)S(1)}, bf16[2,128,4,192]{1,0,3,2:T(2,128)(2,1)}, u32[]{:S(2)}) copy-start(bf16[2,128,4,192]{1,0,3,2:T(2,128)(2,1)} %copy.27) | copy-start | bytes 1179652
  162.6 26.2 %copy-start.36 = (f32[256]{0:T(256)S(1)}, f32[256]{0:T(256)}, u32[]{:S(2)}) copy-start(f32[256]{0:T(256)} %copy-done.34) | copy-start | bytes 3076
  196.1 91.6 %copy-start.16 = (f32[256,768]{1,0:T(8,128)S(1)}, f32[256,768]{1,0:T(8,128)}, u32[]{:S(2)}) copy-start(f32[256,768]{1,0:T(8,128)} %copy-done.15) | copy-start | bytes 2359300
  287.7 6.3 %copy-start.26 = (f32[24,3072]{1,0:T(8,128)S(1)}, f32[24,3072]{1,0:T(8,128)}, u32[]{:S(2)}) copy-start(f32[24,3072]{1,0:T(8,128)} %get-tuple-element.93) | copy-start | bytes 884740
  287.7 7.0 %copy-start.25 = (f32[96,768]{1,0:T(8,128)S(1)}, f32[96,768]{1,0:T(8,128)}, u32[]{:S(2)}) copy-start(f32[96,768]{1,0:T(8,128)} %get-tuple-element.95) | copy-start | bytes 884740
  (24 other events, 54.7 us)
